TPU v7x, 256 devices: a whole 4x4x8 slice. The times are simulated.
256 devices in a mesh: dp: 4 (over y), shard: 64 (over x, z, core).
Axes of the slice: x: 4, y: 4, z: 8, core: 2. Of those that a mesh axis runs over, the one named last changes fastest.
Arguments:
- training_inputs: bfloat16 [32768, 8192], P(('dp', 'shard')), may hold values from -6 to 6
- training_cotangents: bfloat16 [32768, 8192], P(('dp', 'shard')), may hold values from -6 to 6
- validation_inputs: bfloat16 [8192, 8192], P(('dp', 'shard')), may hold values from -6 to 6
- validation_cotangents: bfloat16 [8192, 8192], P(('dp', 'shard')), may hold values from -6 to 6
- adapter_down: bfloat16 [8192, 64], replicated, may hold values from -0.0625 to 0.0625
- adapter_up: bfloat16 [64, 8192], replicated, may hold values from -0.0625 to 0.0625
- adam_first_moment: bfloat16 [64, 128, 128], P('shard'), may hold values from -6 to 6
- adam_second_moment: bfloat16 [64, 128, 128], P('shard'), may hold values from 0.019897461 to 20
- slot_block_index: int32 [64], replicated, may hold values from 0 to 63, each once
- example_lengths: int32 [4, 64, 8], P('dp', 'shard'), may hold values from 1 to 64, 128 in all within a row
- projection_rows: float32 [128, 64], replicated, may hold values from -0.5 to 0.5
- projection_columns: float32 [8192, 128], replicated, may hold values from -0.0625 to 0.0625
Outputs:
- train_dirs: float32 [4, 64, 8, 8192], P('dp', 'shard')
- val_dir: float32 [8192], replicated
- scores: float32 [4, 64, 8], P('dp', 'shard')
Inputs may be any that keep to these rules, and one draw needn't show every extreme that they name: slot_block_index holds every block number once. `example_lengths`: each device's 8 lengths sum to 128; on every device the longest example has exactly 64 tokens.
All inputs are finite; a program needn't handle non-finite values.
Results may differ from a plain program's by a relative error of at most 0.015.
Values may be sent and summed in bfloat16 or wider, within the bound.
A program may use at most 192 MiB of HBM per device.

v0:
```python
import math

import jax
import jax.numpy as jnp
from jax import lax
from jax.sharding import PartitionSpec as P

beta_first = 0.9
beta_second = 0.999
epsilon = 1e-06


def membership(lengths, total_rows):
    finish = jnp.cumsum(lengths)
    begins = finish - lengths
    position = jnp.arange(total_rows, dtype=jnp.int32)[:, None]
    return ((position >= begins[None, :]) & (position < finish[None, :])).astype(jnp.bfloat16)


def reduced_rank(input_rows, output_cotangent, adapter_down, adapter_up):
    backward_adapter = jnp.dot(
        output_cotangent, adapter_up.T, preferred_element_type=jnp.float32
    ).astype(jnp.bfloat16)
    forward_adapter = jnp.dot(input_rows, adapter_down, preferred_element_type=jnp.float32).astype(
        jnp.bfloat16
    )
    return (backward_adapter, forward_adapter)


def normalize(vector):
    return vector / jnp.sqrt(jnp.mean(vector * vector, axis=-1, keepdims=True) + epsilon)


def project(gradient, projection_rows, columns):
    inner = jnp.dot(gradient, columns, precision=lax.Precision.HIGHEST)
    return jnp.einsum("rj,rk->jk", projection_rows, inner, precision=lax.Precision.HIGHEST)


def token_sum(masked, values):
    return lax.dot_general(
        masked, values, (((0,), (0,)), ((), ())), preferred_element_type=jnp.float32
    )


def body(
    training_inputs,
    training_cotangents,
    validation_inputs,
    validation_cotangents,
    adapter_down,
    adapter_up,
    adam_first_moment,
    adam_second_moment,
    slot_block_index,
    example_lengths,
    projection_rows,
    projection_columns,
):
    local_tokens = training_inputs.shape[0]
    adapter_rank = adapter_down.shape[1]
    example_rows = example_lengths.shape[2]
    block_count = slot_block_index.shape[0]
    block_span_width = adam_first_moment.shape[2]
    table_width = projection_columns.shape[1]
    backward_adapter, forward_adapter = reduced_rank(
        training_inputs, training_cotangents, adapter_down, adapter_up
    )
    member_flag = membership(example_lengths[0, 0], local_tokens)
    masked_backward = (backward_adapter[:, None, :] * member_flag[:, :, None]).reshape(
        local_tokens, example_rows * adapter_rank
    )
    forward_masked = (forward_adapter[:, None, :] * member_flag[:, :, None]).reshape(
        local_tokens, example_rows * adapter_rank
    )
    input_blocks = training_inputs.reshape(local_tokens, block_count, block_span_width)
    cotangent_blocks = training_cotangents.reshape(local_tokens, block_count, block_span_width)
    col_tables = projection_columns.reshape(block_count, block_span_width, table_width)
    first_stat = lax.all_gather(adam_first_moment, "shard", axis=0, tiled=True)
    second_stat = lax.all_gather(adam_second_moment, "shard", axis=0, tiled=True)
    segment_count = first_stat.shape[0]
    input_rows = jnp.take(input_blocks, slot_block_index, axis=1).reshape(
        local_tokens, segment_count * block_span_width
    )
    output_cotangent = jnp.take(cotangent_blocks, slot_block_index, axis=1).reshape(
        local_tokens, segment_count * block_span_width
    )
    top_half = token_sum(masked_backward, input_rows).reshape(
        example_rows, adapter_rank, segment_count, block_span_width
    )
    bottom_half = token_sum(forward_masked, output_cotangent).reshape(
        example_rows, adapter_rank, segment_count, block_span_width
    )
    gradient = jnp.concatenate([top_half, bottom_half], axis=1)
    first_part = first_stat.astype(jnp.float32).transpose(1, 0, 2)[None]
    second_part = second_stat.astype(jnp.float32).transpose(1, 0, 2)[None]
    update = (beta_first * first_part + (1 - beta_first) * gradient) / jnp.sqrt(
        beta_second * second_part + (1 - beta_second) * gradient * gradient
    )
    tables = jnp.take(col_tables, slot_block_index, axis=0)
    folded = jnp.einsum("erny,nyk->erk", update, tables, precision=lax.Precision.HIGHEST)
    projected = jnp.einsum("rj,erk->ejk", projection_rows, folded, precision=lax.Precision.HIGHEST)
    directions = normalize(projected.reshape(example_rows, -1))
    validation_backward, validation_forward = reduced_rank(
        validation_inputs, validation_cotangents, adapter_down, adapter_up
    )
    local_grad = jnp.concatenate(
        [
            token_sum(validation_backward, validation_inputs),
            token_sum(validation_forward, validation_cotangents),
        ],
        axis=0,
    )
    summed = lax.psum(local_grad, ("dp", "shard"))
    val_proj = project(summed, projection_rows, projection_columns)
    val_dir = normalize(val_proj.reshape(-1))
    scores = jnp.sum(directions * val_dir, axis=-1) / math.sqrt(directions.shape[-1])
    return (directions[None, None], val_dir, scores[None, None])


def solution(mesh):
    return jax.shard_map(
        body,
        mesh=mesh,
        in_specs=(
            P(("dp", "shard"), None),
            P(("dp", "shard"), None),
            P(("dp", "shard"), None),
            P(("dp", "shard"), None),
            P(),
            P(),
            P("shard", None, None),
            P("shard", None, None),
            P(),
            P("dp", "shard", None),
            P(),
            P(),
        ),
        out_specs=(P("dp", "shard", None, None), P(), P("dp", "shard", None)),
        check_vma=False,
    )
```

profile of v0, /device:TPU:2, one launch (start us, length us, event | category | flops | bytes accessed | tf_op | source)
XLA Modules:
  0.0 370.5 jit_solution(9689042469179392533)
XLA Ops:
  8.1 3.0 fusion.24
  11.0 3.9 %fusion.25 = f32[64,8192]{1,0:T(8,128)} fusion(bf16[32,8192]{1,0:T(8,128)(2,1)} %param.17, bf16[32,8192]{1,0:T(8,128)(2,1)} %param.16, bf16[8192,64]{0,1:T(8,128)(2,1)S(1)} %copy-done), kind=kOutput, calls=%fused_computation.35 | convolution fusion | flops 67110912 | bytes 4194304 | tf_op jit(solution)/shard_map/dot_general | solution.py:40
  15.0 4.1 %pad_maximum_fusion.2 = f32[128,8192]{1,0:T(8,128)} fusion(f32[64,8192]{1,0:T(8,128)} %fusion.25, f32[64,8192]{1,0:T(8,128)S(1)} %fusion.24), kind=kLoop, calls=%fused_computation.15 | loop fusion | flops 1048576 | bytes 8388608 | tf_op jit(solution)/shard_map/concatenate | solution.py:106
  19.1 0.5 all-gather.5.cloned.1.call-update
  19.7 0.5 all-gather.3.cloned.1.call-update
  20.3 0.4 copy-done.3
  20.6 2.4 copy.23
  23.0 4.2 %copy.24 = bf16[128,64,128]{2,0,1:T(8,128)(2,1)} copy(bf16[128,64,128]{0,2,1:T(8,128)(2,1)} %bitcast.94) | data formatting | bytes 4194304 | tf_op jit(solution)/shard_map/reshape | solution.py:75
  27.3 2.4 copy.26
  29.7 4.2 %copy.27 = bf16[128,64,128]{2,0,1:T(8,128)(2,1)} copy(bf16[128,64,128]{0,2,1:T(8,128)(2,1)} %bitcast.95) | data formatting | bytes 4194304 | tf_op jit(solution)/shard_map/reshape | solution.py:76
  33.9 2.2 gather_fusion.1
  36.1 3.9 %gather_fusion.2 = bf16[64,128,128]{2,1,0:T(8,128)(2,1)} fusion(bf16[128,64,128]{2,0,1:T(8,128)(2,1)} %copy.27, s32[1024]{0:T(1024)S(1)} %pad_clamp_fusion), kind=kCustom, calls=%fused_computation.1.clone | custom fusion | bytes 4194560 | tf_op jit(solution)/shard_map/jit(_take)/gather | solution.py:84
  40.0 4.1 %select_bitcast_fusion.1 = (bf16[128,64,128]{2,0,1:T(8,128)(2,1)}, bf16[128,64,128]{2,0,1:T(8,128)(2,1)}) fusion(bf16[64,128,128]{2,1,0:T(8,128)(2,1)S(1)} %copy-done.6, pred[64]{0:T(512)(128)(4,1)S(1)} %compare_and_fusion, bf16[64,128,128]{2,1,0:T(8,128)(2,1)} %gather_fusion.2), kind=kLoop, calls=%fused_computation.25 | loop fusion | flops 2097152 | bytes 8388672 | tf_op jit(solution)/shard_map/jit(_take)/select_n | solution.py:81
  44.1 3.2 copy.28
  47.3 4.1 %copy.25 = bf16[128,64,128]{0,2,1:T(8,128)(2,1)} copy(bf16[128,64,128]{2,0,1:T(8,128)(2,1)} %get-tuple-element.6) | data formatting | bytes 4194304 | tf_op jit(solution)/shard_map/jit(_take)/select_n | solution.py:81
  51.4 5.0 %gather_fusion = f32[64,128,128]{2,1,0:T(8,128)} fusion(f32[64,128,128]{2,1,0:T(8,128)} %bitcast.93, s32[1024]{0:T(1024)S(1)} %pad_clamp_fusion), kind=kCustom, calls=%fused_computation.2 | custom fusion | bytes 8388864 | tf_op jit(solution)/shard_map/jit(_take)/gather | solution.py:99
  56.5 0.2 reduce-window.7
  56.7 2.4 convolution_convert_fusion
  59.2 2.7 convolution_convert_fusion.1
  61.9 8.1 %fusion.13 = f32[8,64,64,128]{3,1,2,0:T(8,128)} fusion(bf16[128,64,128]{0,2,1:T(8,128)(2,1)S(1)} %copy.28, bf16[128,64]{0,1:T(8,128)(2,1)S(1)} %convolution_convert_fusion, bf16[128,8]{0,1:T(8,128)(2,1)S(1)} %fusion.38), kind=kOutput, calls=%fused_computation.20 | convolution fusion | flops 1074003968 | bytes 18892800 | tf_op jit(solution)/shard_map/dot_general | solution.py:40
  70.0 8.1 %fusion.15 = f32[8,64,64,128]{3,1,2,0:T(8,128)} fusion(bf16[128,64,128]{0,2,1:T(8,128)(2,1)S(1)} %copy-done.2, bf16[128,8]{0,1:T(8,128)(2,1)S(1)} %fusion.38, bf16[128,64]{0,1:T(8,128)(2,1)S(1)} %convolution_convert_fusion.1), kind=kOutput, calls=%fused_computation.22 | convolution fusion | flops 1074003968 | bytes 18892800 | tf_op jit(solution)/shard_map/dot_general | solution.py:40
  78.1 214.8 %all-reduce.2.cloned.1.call-done = f32[128,8192]{1,0:T(8,128)} async-done(((f32[128,8192]{1,0:T(8,128)}), f32[128,8192]{1,0:T(8,128)}) %all-reduce.2.cloned.1.call-update) | async-done | bytes 4194320 | tf_op jit(solution)/shard_map/psum | solution.py:113
  292.9 7.6 %fusion.43 = f32[128,128]{1,0:T(8,128)S(1)} fusion(f32[128,8192]{1,0:T(8,128)} %all-reduce.2.cloned.1.call-done, f32[8192,128]{1,0:T(8,128)} %param.25), kind=kOutput, calls=%fused_computation.66 | convolution fusion | flops 1610612736 | bytes 8454144 | tf_op jit(solution)/shard_map/dot_general | solution.py:35
  300.5 0.8 multiply_reduce_fusion.2
  302.0 0.6 fusion.36
  302.6 4.2 %multiply_bitcast_fusion = f32[128,64,128]{2,0,1:T(8,128)} fusion(bf16[64,128,128]{2,1,0:T(8,128)(2,1)} %all-gather.5.cloned.1.call-done), kind=kLoop, calls=%fused_computation.18 | loop fusion | flops 2097152 | bytes 6291456 | tf_op jit(solution)/shard_map/mul | solution.py:97
  306.9 4.1 %multiply_bitcast_fusion.1 = f32[128,64,128]{2,0,1:T(8,128)} fusion(bf16[64,128,128]{2,1,0:T(8,128)(2,1)} %all-gather.3.cloned.1.call-done), kind=kLoop, calls=%fused_computation.19 | loop fusion | flops 2097152 | bytes 6291456 | tf_op jit(solution)/shard_map/mul | solution.py:96
  311.0 49.9 %fusion.19 = f32[8,128,128]{2,1,0:T(8,128)S(1)} fusion(f32[64,128,128]{2,1,0:T(8,128)} %gather_fusion, pred[64]{0:T(512)(128)(4,1)S(1)} %compare_and_fusion, f32[8,64,64,128]{3,1,2,0:T(8,128)} %fusion.13, f32[8,64,64,128]{3,1,2,0:T(8,128)} %fusion.15, f32[128,64,128]{2,0,1:T(8,128)} %multiply_bitcast_fusion, f32[128,64,128]{2,0,1:T(8,128)} %multiply_bitcast_fusion.1), kind=kOutput, calls=%fused_computation.28 | convolution fusion | flops 12944670720 | bytes 46661696 | tf_op jit(solution)/shard_map/erny,nyk->erk/dot_general | solution.py:100
  360.9 0.5 multiply_reduce_fusion.1
  361.5 0.2 multiply_reduce_fusion
  361.7 0.5 multiply_bitcast_fusion.2
  362.2 0.8 broadcast_divide_fusion
  (32 shorter events, 0.4 us)
Async XLA Ops:
  8.0 3.0 copy-start
  8.0 284.9 %all-reduce.2.cloned.1.call-start = ((), (), s32[]{:S(2)}) async-start(), calls=%async_computation.2 | async-start | bytes 8388608 | tf_op jit(solution)/shard_map/psum | solution.py:113
  19.0 1.2 copy-start.8
  19.0 1.6 copy-start.3
  19.0 283.6 %all-gather.5.cloned.1.call-start = ((), (), s32[]{:S(2)}) async-start(), calls=%async_computation.1 | async-start | bytes 2129920 | tf_op jit(solution)/shard_map/all_gather | solution.py:79
  19.6 287.2 %all-gather.3.cloned.1.call-start = ((), (), s32[]{:S(2)}) async-start(), calls=%async_computation | async-start | bytes 2129920 | tf_op jit(solution)/shard_map/all_gather | solution.py:78
  23.0 4.2 %copy-start.4 = (bf16[128,8192]{1,0:T(8,128)(2,1)S(1)}, bf16[128,8192]{1,0:T(8,128)(2,1)}, u32[]{:S(2)}) copy-start(bf16[128,8192]{1,0:T(8,128)(2,1)} %param.15) | copy-start | bytes 6291460
  29.7 4.2 %copy-start.5 = (bf16[128,64,128]{2,0,1:T(8,128)(2,1)S(1)}, bf16[128,64,128]{2,0,1:T(8,128)(2,1)}, u32[]{:S(2)}) copy-start(bf16[128,64,128]{2,0,1:T(8,128)(2,1)} %copy.24) | copy-start | bytes 6291460
  36.1 3.9 %copy-start.6 = (bf16[64,128,128]{2,1,0:T(8,128)(2,1)S(1)}, bf16[64,128,128]{2,1,0:T(8,128)(2,1)}, u32[]{:S(2)}) copy-start(bf16[64,128,128]{2,1,0:T(8,128)(2,1)} %gather_fusion.1) | copy-start | bytes 6291460
  51.4 5.0 %copy-start.9 = (s32[1,1,8]{2,1,0:T(1,128)S(1)}, s32[1,1,8]{2,1,0:T(1,128)}, u32[]{:S(2)}) copy-start(s32[1,1,8]{2,1,0:T(1,128)} %param.23) | copy-start | bytes 100
  61.9 8.1 %copy-start.2 = (bf16[128,64,128]{0,2,1:T(8,128)(2,1)S(1)}, bf16[128,64,128]{0,2,1:T(8,128)(2,1)}, u32[]{:S(2)}) copy-start(bf16[128,64,128]{0,2,1:T(8,128)(2,1)} %copy.25) | copy-start | bytes 6291460
  78.1 222.4 %copy-start.7 = (f32[128,64]{0,1:T(8,128)S(1)}, f32[128,64]{0,1:T(8,128)}, u32[]{:S(2)}) copy-start(f32[128,64]{0,1:T(8,128)} %param.24) | copy-start | bytes 98308
  311.0 52.0 %copy-start.1 = (bf16[8192,64]{0,1:T(8,128)(2,1)S(1)}, bf16[8192,64]{0,1:T(8,128)(2,1)}, u32[]{:S(2)}) copy-start(bf16[8192,64]{0,1:T(8,128)(2,1)} %param.18) | copy-start | bytes 3145732
Sparse Core Ops, SparseCore 0:
  19.2 273.6 all-reduce.1
Sparse Core Ops, SparseCore 1:
  22.3 79.9 all-gather.4
  104.9 75.1 all-gather.2
where the time goes:
time: 371 us; the launch traced here: 370 us
  waiting for transfers between devices  216 us (58%)
  matrix products  87.1 us (23%)
  local copies, waits for them, and re-layouts  32.2 us (9%)
  other arithmetic  18.9 us (5%)
  between operations  16.3 us (4%)
    psum x1, waiting for transfers between devices, body(): summed = lax.psum(local_grad, ('dp', 'shard'))  215 us
    dot_general x1, matrix products, body(): jnp.einsum('erny,nyk->erk', update, tables, precision=lax.Precision.HIGHEST)  49.9 us
    dot_general x4, matrix products, token_sum(): lax.dot_general(masked, values, (((0,), (0,)), ((), ())), preferred_eleme...  23.1 us
    dot_general x1, matrix products, project(): inner = jnp.dot(gradient, columns, precision=lax.Precision.HIGHEST)  7.62 us
  transfers between devices with their start and end apart: 3, of which 1 were waited for; matrix products, arithmetic and copies ran while one was open for 19% of the time, Pallas kernels for 0%

commit v1 on v0

v1 whole, which is shorter than its diff:
```python
import math

import jax
import jax.numpy as jnp
from jax import lax
from jax.experimental import pallas as pl
from jax.experimental.pallas import tpu as pltpu
from jax.sharding import PartitionSpec as P

NX, NY, NZ = 4, 4, 8
SLOTS = 2 * NX * NZ
PAIRS = SLOTS // 2
LEAD = 9
W = 128
RANK = 64
EXAMPLES = 8
WIDTH = 8192
TOKENS = 128
VAL = 32
CHUNK = 1024

beta_first = 0.9
beta_second = 0.999
epsilon = 1e-06
FIRST = beta_first / (1 - beta_first)
SECOND = beta_second / (1 - beta_second)
GAIN = (1 - beta_first) / math.sqrt(1 - beta_second)

MESH = pl.DeviceIdType.MESH
HIGHEST = lax.Precision.HIGHEST


def offset(i):
    return ((i + 1) // 2) * (1 - 2 * (i % 2))


def even_order(k):
    late = (k >= 8).astype(jnp.int32)
    last = (k >= 24).astype(jnp.int32)
    g = late * (1 - last) * (1 + k % 2) + last * 3
    j = (1 - late) * k + late * (1 - last) * ((k - 8) // 2) + last * (k - 24)
    return g, j


def odd_order(k):
    late = (k >= 4).astype(jnp.int32)
    last = (k >= 28).astype(jnp.int32)
    hop = 1 + (k - 4) // 8
    i = (k + 4) % 8
    g = (1 - late) * k + late * (1 - last) * (i // 2) + last * (k - 28)
    j = late * (1 - last) * (2 * hop - 1 + i % 2) + last * 7
    return g, j


def split(a):
    high = a.astype(jnp.bfloat16)
    return high, (a - high.astype(jnp.float32)).astype(jnp.bfloat16)


def nt(a, b):
    return lax.dot_general(a, b, (((1,), (1,)), ((), ())), preferred_element_type=jnp.float32)


def prepare(
    x_hbm, ct_hbm, xv_hbm, ctv_hbm, down_hbm, up_hbm, pc_hbm, rt_ref, blocks, lengths,
    x_slots, ct_slots, table_slots, masked, val_part,
    xs, cts, xvs, ctvs, downs, ups, pcs, load_sem,
):
    loads = [
        pltpu.make_async_copy(a, b, load_sem.at[i])
        for i, (a, b) in enumerate(
            [(up_hbm, ups), (ct_hbm, cts), (down_hbm, downs), (x_hbm, xs), (pc_hbm, pcs), (xv_hbm, xvs), (ctv_hbm, ctvs)]
        )
    ]
    for copy in loads:
        copy.start()

    def reduced(weights, rows, count):
        def step(i, total_):
            cols = pl.ds(pl.multiple_of(i * CHUNK, CHUNK), CHUNK)
            return total_ + nt(weights[:, cols], rows[:, cols])

        return lax.fori_loop(0, WIDTH // CHUNK, step, jnp.zeros((RANK, count), jnp.float32)).astype(jnp.bfloat16)

    lane = lax.broadcasted_iota(jnp.int32, (RANK, TOKENS), 1)

    def mask(half, adapted):
        begin = jnp.int32(0)
        for e in range(EXAMPLES):
            finish = begin + lengths[e]
            inside = (lane >= begin) & (lane < finish)
            masked[half, e * RANK : (e + 1) * RANK, :] = jnp.where(inside, adapted.astype(jnp.float32), 0.0).astype(jnp.bfloat16)
            begin = finish

    loads[0].wait()
    loads[1].wait()
    mask(0, reduced(ups, cts, TOKENS))
    loads[2].wait()
    loads[3].wait()
    mask(1, reduced(downs, xs, TOKENS))
    for i in (4, 5, 6):
        loads[i].wait()
    vback = reduced(ups, ctvs, VAL)
    vfwd = reduced(downs, xvs, VAL)

    def val_step(i, carry):
        a, b = carry
        cols = pl.ds(pl.multiple_of(i * CHUNK, CHUNK), CHUNK)
        for part in split(pcs[cols, :]):
            a = a + jnp.dot(xvs[:, cols], part, preferred_element_type=jnp.float32)
            b = b + jnp.dot(ctvs[:, cols], part, preferred_element_type=jnp.float32)
        return a, b

    zero = jnp.zeros((VAL, W), jnp.float32)
    in_cols, ct_cols = lax.fori_loop(0, WIDTH // CHUNK, val_step, (zero, zero))
    val_inner = jnp.concatenate(
        [
            jnp.dot(vback.astype(jnp.float32), in_cols, precision=HIGHEST, preferred_element_type=jnp.float32),
            jnp.dot(vfwd.astype(jnp.float32), ct_cols, precision=HIGHEST, preferred_element_type=jnp.float32),
        ],
        axis=0,
    )
    val_part[...] = jnp.dot(rt_ref[...], val_inner, precision=HIGHEST, preferred_element_type=jnp.float32)

    def reorder(i, _):
        for j in range(4):
            slot = 4 * i + j
            columns = pl.ds(pl.multiple_of(blocks[slot] * W, W), W)
            x_slots[slot] = xs[:, columns]
            ct_slots[slot] = cts[:, columns]
            for i_part, part in enumerate(split(pcs[columns, :])):
                table_slots[slot, i_part] = part
        return 0

    lax.fori_loop(0, SLOTS // 4, reorder, 0)


def kernel(
    m_hbm, v_hbm, x_slots, ct_slots, table_slots, masked, val_part, rt_ref,
    dirs_ref, vdir_ref, scores_ref,
    mom, acc, red_c, red_y, red_x, red_z,
    own_sem, recv, send, rc_recv, ry_recv, rx_recv, rz_recv, rc_send, ry_send, rx_send, rz_send,
):
    me = lax.axis_index("shard")
    my_y = lax.axis_index("dp")
    core = me % 2
    my_z = (me // 2) % NZ
    my_x = me // (2 * NZ)

    def place(x, z, c):
        return (x * NZ + z) * 2 + c

    partner = place(my_x, my_z, 1 - core)

    own_copies = [
        pltpu.make_async_copy(m_hbm.at[0], mom.at[me, 0], own_sem.at[0]),
        pltpu.make_async_copy(v_hbm.at[0], mom.at[me, 1], own_sem.at[1]),
    ]
    barrier = pltpu.get_barrier_semaphore()

    def greet(axis, peer):
        pl.semaphore_signal(barrier, inc=1, device_id={axis: peer}, device_id_type=MESH)

    for d in range(1, NZ):
        greet("shard", place(my_x, (my_z + d) % NZ, core))
    for d in range(1, NX):
        greet("shard", place((my_x + d) % NX, my_z, core))
    for d in range(1, NY):
        greet("dp", (my_y + d) % NY)
    greet("shard", partner)
    for copy in own_copies:
        copy.start()
    for copy in own_copies:
        copy.wait()
    pl.semaphore_wait(barrier, NZ + NX + NY - 3 + 1)

    def slot_copy(slot, k, way, peer):
        return pltpu.make_async_remote_copy(
            src_ref=mom.at[slot],
            dst_ref=mom.at[slot],
            send_sem=send.at[k, way],
            recv_sem=recv.at[slot],
            device_id={"shard": peer},
            device_id_type=MESH,
        )

    def even_slot(k):
        g, j = even_order(k)
        return place((my_x + offset(g) + NX) % NX, (my_z + offset(j) + NZ) % NZ, 0)

    def odd_slot(k):
        g, j = odd_order(k)
        return place((my_x + offset(g) + NX) % NX, (my_z + offset(j) + NZ) % NZ, 1)

    def sends(k, act):
        x_up, x_down = place((my_x + 1) % NX, my_z, core), place((my_x + NX - 1) % NX, my_z, core)
        z_up, z_down = place(my_x, (my_z + 1) % NZ, core), place(my_x, (my_z + NZ - 1) % NZ, core)

        def go(cond, slot, way, peer):
            @pl.when(cond)
            def _():
                act(slot_copy(slot, k, way, peer))

        @pl.when(core == 0)
        def _():
            slot = even_slot(k)
            first, second = k < 8, (k >= 8) & (k < 24)
            g, j = even_order(k)
            go(first & ((k == 0) | ((k % 2 == 1) & (k <= 5))), slot, 0, z_up)
            go(first & ((k % 2 == 0) & (k <= 4)), slot, 1, z_down)
            go(first | (second & (g == 1) & (j % 2 == 0)), slot, 2, x_up)
            go(first | (second & (g == 2) & (j % 2 == 1)), slot, 3, x_down)
            act(slot_copy(slot, k, 4, partner))

        @pl.when(core == 1)
        def _():
            slot = odd_slot(k)
            first, second = k < 4, (k >= 4) & (k < 28)
            g, j = odd_order(k)
            go(first | (second & (j % 2 == 1) & ((j <= 3) | (g % 2 == 0))), slot, 0, z_up)
            go(first | (second & (j % 2 == 0) & ((j <= 4) | (g % 2 == 1))), slot, 1, z_down)
            go(first & (k <= 1), slot, 2, x_up)
            go(k == 0, slot, 3, x_down)
            act(slot_copy(slot, k, 4, partner))

    def arrive(k):
        slot = (1 - core) * even_slot(k) + core * odd_slot(k)
        slot_copy(slot, k, 4, partner).wait_recv()
        sends(k, lambda copy: copy.start())

    def spread(buffer, mine, peers, send_sems, recv_sems, axis, act):
        for i, (peer, theirs) in enumerate(peers):
            source = theirs if act == "wait" else mine
            copy = pltpu.make_async_remote_copy(
                src_ref=buffer.at[source],
                dst_ref=buffer.at[source],
                send_sem=send_sems.at[i],
                recv_sem=recv_sems.at[source],
                device_id={axis: peer},
                device_id_type=MESH,
            )
            if act == "start":
                copy.start()
            elif act == "sent":
                copy.wait_send()
            else:
                copy.wait_recv()

    def stage(name, act):
        if name == "core":
            spread(red_c, core, [(partner, 1 - core)], rc_send, rc_recv, "shard", act)
        elif name == "y":
            there = [(my_y + d) % NY for d in range(1, NY)]
            spread(red_y, my_y, [(t, t) for t in there], ry_send, ry_recv, "dp", act)
        elif name == "x":
            there = [(my_x + d) % NX for d in range(1, NX)]
            spread(red_x, my_x, [(place(t, my_z, core), t) for t in there], rx_send, rx_recv, "shard", act)
        else:
            there = [(my_z + d) % NZ for d in range(1, NZ)]
            spread(red_z, my_z, [(place(my_x, t, core), t) for t in there], rz_send, rz_recv, "shard", act)

    def total(buffer, count):
        out = buffer[0]
        for i in range(1, count):
            out = out + buffer[i]
        return out

    const = lambda i: jnp.int32(i)
    sends(const(0), lambda copy: copy.start())

    red_c[core] = val_part[...]
    acc[...] = jnp.zeros_like(acc)

    def pair(k, _):
        @pl.when(k < LEAD - 1)
        def _():
            arrive(2 * k + 1)
            arrive(2 * k + 2)

        @pl.when((k >= LEAD - 1) & (k < PAIRS - LEAD))
        def _():
            arrive(k + LEAD)

        @pl.when(k == 0)
        def _():
            stage("core", "start")

        @pl.when(k == 2)
        def _():
            stage("core", "wait")
            red_y[my_y] = total(red_c, 2)

        @pl.when(k == 3)
        def _():
            stage("y", "start")

        @pl.when(k == 7)
        def _():
            stage("y", "wait")
            red_x[my_x] = total(red_y, NY)

        @pl.when(k == 8)
        def _():
            stage("x", "start")

        @pl.when(k == 12)
        def _():
            stage("x", "wait")
            red_z[my_z] = total(red_x, NX)

        @pl.when(k == 13)
        def _():
            stage("z", "start")

        slots = [even_slot(k), odd_slot(k)]
        theirs = core * slots[0] + (1 - core) * slots[1]
        slot_copy(theirs, k, 4, partner).wait_recv()
        table = jnp.concatenate([table_slots[s, part] for part in range(2) for s in slots], axis=0)
        for half, rows in ((0, x_slots), (1, ct_slots)):
            right = jnp.concatenate([rows[s] for s in slots], axis=1)
            grad = jnp.dot(masked[half], right, preferred_element_type=jnp.float32)
            span = slice(half * RANK, (half + 1) * RANK)
            first = FIRST * jnp.concatenate([mom[s, 0, span, :] for s in slots], axis=1).astype(jnp.float32)
            second = SECOND * jnp.concatenate([mom[s, 1, span, :] for s in slots], axis=1).astype(jnp.float32)
            parts = []
            for e in range(EXAMPLES):
                g = grad[e * RANK : (e + 1) * RANK]
                parts.append(((first + g) * lax.rsqrt(second + g * g)).astype(jnp.bfloat16))
            update = jnp.concatenate(parts, axis=0)
            acc[half] += jnp.dot(jnp.concatenate([update, update], axis=1), table, preferred_element_type=jnp.float32)
        return 0

    lax.fori_loop(0, PAIRS, pair, 0)

    stage("z", "wait")
    val_proj = total(red_z, NZ)
    val_dir = val_proj / jnp.sqrt(jnp.sum(val_proj * val_proj, keepdims=True) / (RANK * W) + epsilon)
    vdir_ref[...] = val_dir
    where = lax.broadcasted_iota(jnp.int32, (1, EXAMPLES), 1)
    scores = jnp.zeros((1, EXAMPLES), jnp.float32)
    for e in range(EXAMPLES):
        rows = slice(e * RANK, (e + 1) * RANK)
        inner = jnp.concatenate([acc[0, rows, :], acc[1, rows, :]], axis=0)
        proj = GAIN * jnp.dot(rt_ref[...], inner, precision=HIGHEST, preferred_element_type=jnp.float32)
        direction = proj / jnp.sqrt(jnp.sum(proj * proj, keepdims=True) / (RANK * W) + epsilon)
        dirs_ref[pl.ds(e, RANK, stride=EXAMPLES), :] = direction
        score = jnp.sum(direction * val_dir, keepdims=True) / math.sqrt(RANK * W)
        scores = scores + jnp.where(where == e, score, 0.0)
    scores_ref[...] = scores

    for name in ("core", "y", "x", "z"):
        stage(name, "sent")

    def drain(k, _):
        sends(k, lambda copy: copy.wait_send())
        return 0

    lax.fori_loop(0, PAIRS, drain, 0)


def body(
    training_inputs,
    training_cotangents,
    validation_inputs,
    validation_cotangents,
    adapter_down,
    adapter_up,
    adam_first_moment,
    adam_second_moment,
    slot_block_index,
    example_lengths,
    projection_rows,
    projection_columns,
):
    hbm = pl.BlockSpec(memory_space=pltpu.MemorySpace.HBM)
    vmem = pl.BlockSpec(memory_space=pltpu.MemorySpace.VMEM)
    smem = pl.BlockSpec(memory_space=pltpu.MemorySpace.SMEM)
    bf16, f32 = jnp.bfloat16, jnp.float32
    dma = pltpu.SemaphoreType.DMA
    rows_t = projection_rows.T
    slots = jax.ShapeDtypeStruct((SLOTS, W, W), bf16)
    x_slots, ct_slots, table_slots, masked, val_part = pl.pallas_call(
        prepare,
        name="prepare",
        out_shape=(
            slots,
            slots,
            jax.ShapeDtypeStruct((SLOTS, 2, W, W), bf16),
            jax.ShapeDtypeStruct((2, EXAMPLES * RANK, TOKENS), bf16),
            jax.ShapeDtypeStruct((RANK, W), f32),
        ),
        in_specs=[hbm] * 7 + [vmem, smem, smem],
        out_specs=(vmem,) * 5,
        scratch_shapes=[
            pltpu.VMEM((TOKENS, WIDTH), bf16),
            pltpu.VMEM((TOKENS, WIDTH), bf16),
            pltpu.VMEM((VAL, WIDTH), bf16),
            pltpu.VMEM((VAL, WIDTH), bf16),
            pltpu.VMEM((RANK, WIDTH), bf16),
            pltpu.VMEM((RANK, WIDTH), bf16),
            pltpu.VMEM((WIDTH, W), f32),
            dma((7,)),
        ],
        compiler_params=pltpu.CompilerParams(vmem_limit_bytes=36 * 1024 * 1024),
    )(
        training_inputs,
        training_cotangents,
        validation_inputs,
        validation_cotangents,
        adapter_down.T,
        adapter_up,
        projection_columns,
        rows_t,
        slot_block_index,
        example_lengths.reshape(EXAMPLES),
    )
    dirs, val_dir, scores = pl.pallas_call(
        kernel,
        name="influence",
        out_shape=(
            jax.ShapeDtypeStruct((EXAMPLES * RANK, W), f32),
            jax.ShapeDtypeStruct((RANK, W), f32),
            jax.ShapeDtypeStruct((1, EXAMPLES), f32),
        ),
        in_specs=[hbm] * 2 + [vmem] * 6,
        out_specs=(vmem, vmem, vmem),
        scratch_shapes=[
            pltpu.VMEM((SLOTS, 2, W, W), bf16),
            pltpu.VMEM((2, EXAMPLES * RANK, W), f32),
            pltpu.VMEM((2, RANK, W), f32),
            pltpu.VMEM((NY, RANK, W), f32),
            pltpu.VMEM((NX, RANK, W), f32),
            pltpu.VMEM((NZ, RANK, W), f32),
            dma((2,)),
            dma((SLOTS,)),
            dma((PAIRS, 5)),
            dma((2,)),
            dma((NY,)),
            dma((NX,)),
            dma((NZ,)),
            dma((1,)),
            dma((NY - 1,)),
            dma((NX - 1,)),
            dma((NZ - 1,)),
        ],
        compiler_params=pltpu.CompilerParams(
            collective_id=0, has_side_effects=True, vmem_limit_bytes=32 * 1024 * 1024
        ),
    )(adam_first_moment, adam_second_moment, x_slots, ct_slots, table_slots, masked, val_part, rows_t)
    dirs = dirs.reshape(RANK, EXAMPLES, W).transpose(1, 0, 2).reshape(1, 1, EXAMPLES, RANK * W)
    return (dirs, val_dir.reshape(RANK * W), scores.reshape(1, 1, EXAMPLES))


def solution(mesh):
    return jax.shard_map(
        body,
        mesh=mesh,
        in_specs=(
            P(("dp", "shard"), None),
            P(("dp", "shard"), None),
            P(("dp", "shard"), None),
            P(("dp", "shard"), None),
            P(),
            P(),
            P("shard", None, None),
            P("shard", None, None),
            P(),
            P("dp", "shard", None),
            P(),
            P(),
        ),
        out_specs=(P("dp", "shard", None, None), P(), P("dp", "shard", None)),
        check_vma=False,
    )
```

time: 371 us -> 79.6 us (0.21)
  waiting for transfers between devices: 216 us -> 0 us
  matrix products: 87.1 us -> 0 us
  Pallas kernels: 0 us -> 66.7 us
  local copies, waits for them, and re-layouts: 32.2 us -> 11.6 us
  other arithmetic: 18.9 us -> 0 us
  between operations: 16.3 us -> 0.69 us
    psum x1 -> x0, waiting for transfers between devices: 215 us -> none  [body(): summed = lax.psum(local_grad, ('dp', 'shard'))]
    dot_general x10 -> x0, matrix products: 87.1 us -> none  [the longest x1 49.9 us: body(): jnp.einsum('erny,nyk->erk', update, tables, precision=lax.Precision.HIGHEST)]
    pallas_call x0 -> x2, Pallas kernels: none -> 66.7 us  [the longest x1 55.4 us: body(): pl.pallas_call(kernel, name='influence', out_shape=(jax.ShapeDtypeStruct(...]
    gather x3 -> x0, local copies, waits for them, and re-layouts: 11.1 us -> none  [the longest x1 5.01 us: body(): tables = jnp.take(col_tables, slot_block_index, axis=0)]
    reshape x3 -> x0, local copies, waits for them, and re-layouts: 8.5 us -> none  [the longest x1 4.24 us: body(): training_inputs.reshape(local_tokens, block_count, block_span_width)]
    mul x2 -> x0, other arithmetic: 8.35 us -> none  [the longest x1 4.23 us: body(): beta_second * second_part + (1 - beta_second) * gradient * gradient]
    select_n x2 -> x0, local copies, waits for them, and re-layouts: 7.35 us -> none  [the longest x1 4.11 us: body(): jnp.take(input_blocks, slot_block_index, axis=1)]
    unnamed x22 -> x25, local copies, waits for them, and re-layouts: 5.25 us -> 11.6 us
  transfers between devices with their start and end apart: 3 -> 0, of which waited for: 1 -> 0; matrix products, arithmetic and copies ran while one was open for 19% -> 0% of each run, Pallas kernels for 0% -> 0%
where the time goes in v1:
time: 79.6 us; the launch traced here: 79 us
  Pallas kernels  66.7 us (84%)
  local copies, waits for them, and re-layouts  11.6 us (15%)
    pallas_call x1, Pallas kernels, body(): pl.pallas_call(kernel, name='influence', out_shape=(jax.ShapeDtypeStruct(...  55.4 us
    unnamed x25, local copies, waits for them, and re-layouts  11.6 us
    pallas_call x1, Pallas kernels, body(): pl.pallas_call(prepare, name='prepare', out_shape=(slots, slots, jax.Shap...  11.3 us

profile of v1, /device:TPU:2, one launch (start us, length us, event | category | flops | bytes accessed | tf_op | source)
XLA Modules:
  0.0 79.0 jit_solution(18237035642033792677)
XLA Ops:
  0.6 0.0 copy-start
  0.6 1.6 %copy-done = bf16[128,8192]{1,0:T(8,128)(2,1)S(1)} copy-done((bf16[128,8192]{1,0:T(8,128)(2,1)S(1)}, bf16[128,8192]{1,0:T(8,128)(2,1)}, u32[]{:S(2)}) %copy-start) | copy-done | bytes 2097176
  2.2 0.0 copy-start.1
  2.2 1.6 %copy-done.1 = bf16[128,8192]{1,0:T(8,128)(2,1)S(1)} copy-done((bf16[128,8192]{1,0:T(8,128)(2,1)S(1)}, bf16[128,8192]{1,0:T(8,128)(2,1)}, u32[]{:S(2)}) %copy-start.1) | copy-done | bytes 2097176
  3.8 0.0 copy-start.2
  3.8 1.2 %copy-done.2 = bf16[8192,64]{0,1:T(8,128)(2,1)S(1)} copy-done((bf16[8192,64]{0,1:T(8,128)(2,1)S(1)}, bf16[8192,64]{0,1:T(8,128)(2,1)}, u32[]{:S(2)}) %copy-start.2) | copy-done | bytes 1048600
  5.0 0.0 copy-start.3
  5.0 1.2 %copy-done.3 = bf16[64,8192]{1,0:T(8,128)(2,1)S(1)} copy-done((bf16[64,8192]{1,0:T(8,128)(2,1)S(1)}, bf16[64,8192]{1,0:T(8,128)(2,1)}, u32[]{:S(2)}) %copy-start.3) | copy-done | bytes 1048600
  6.3 0.0 copy-start.4
  6.3 1.0 %copy-done.4 = bf16[32,8192]{1,0:T(8,128)(2,1)S(1)} copy-done((bf16[32,8192]{1,0:T(8,128)(2,1)S(1)}, bf16[32,8192]{1,0:T(8,128)(2,1)}, u32[]{:S(2)}) %copy-start.4) | copy-done | bytes 524312
  7.3 0.0 copy-start.5
  7.3 1.0 %copy-done.5 = bf16[32,8192]{1,0:T(8,128)(2,1)S(1)} copy-done((bf16[32,8192]{1,0:T(8,128)(2,1)S(1)}, bf16[32,8192]{1,0:T(8,128)(2,1)}, u32[]{:S(2)}) %copy-start.5) | copy-done | bytes 524312
  8.4 0.0 copy-start.6
  8.4 0.8 copy-done.6
  9.1 0.0 copy-start.9
  9.1 0.7 copy-done.9
  9.8 0.0 copy-start.10
  9.8 0.7 copy-done.10
  10.4 0.0 copy-start.7
  10.4 0.0 copy-start.8
  10.4 11.3 %prepare.1 = (bf16[64,128,128]{2,1,0:T(8,128)(2,1)S(1)}, bf16[64,128,128]{2,1,0:T(8,128)(2,1)S(1)}, bf16[64,2,128,128]{3,2,1,0:T(8,128)(2,1)S(1)}, bf16[2,512,128]{2,1,0:T(8,128)(2,1)S(1)}, f32[64,128]{1,0:T(8,128)S(1)}) custom-call(bf16[128,8192]{1,0:T(8,128)(2,1)S(1)} %copy-done, bf16[128,8192]{1,0:T(8,128)(2,1)S(1)} %copy-done.1, ...), custom_call_target="tpu_custom_call" | custom-call | tf_op jit(solution)/shard_map/prepare/pallas_call | solution.py:382
  21.7 0.0 copy-done.7
  21.7 0.0 copy-done.8
  21.7 55.4 %influence.1 = (f32[512,128]{1,0:T(8,128)S(1)}, f32[64,128]{1,0:T(8,128)S(1)}, f32[1,8]{1,0:T(1,128)S(1)}) custom-call(bf16[1,128,128]{2,1,0:T(8,128)(2,1)S(1)} %copy-done.7, bf16[1,128,128]{2,1,0:T(8,128)(2,1)S(1)} %copy-done.8, bf16[64,128,128]{2,1,0:T(8,128)(2,1)S(1)} %get-tuple-element.11.x_slots, bf16[64,128,128]{2,1,0:T(8,128)(2,1)S(1)} %get-tuple-element.12.ct_slots, ...), custom_call_target="tpu_custom_call" | custom-call | tf_op jit(solution)/shard_map/influence/pallas_call | solution.py:417
  77.2 0.7 copy.18
  77.9 0.6 copy.19
  78.5 0.5 copy.20
Async XLA Ops:
  0.6 1.6 %copy-start = (bf16[128,8192]{1,0:T(8,128)(2,1)S(1)}, bf16[128,8192]{1,0:T(8,128)(2,1)}, u32[]{:S(2)}) copy-start(bf16[128,8192]{1,0:T(8,128)(2,1)} %x_hbm.1) | copy-start | bytes 6291460
  2.2 1.6 %copy-start.1 = (bf16[128,8192]{1,0:T(8,128)(2,1)S(1)}, bf16[128,8192]{1,0:T(8,128)(2,1)}, u32[]{:S(2)}) copy-start(bf16[128,8192]{1,0:T(8,128)(2,1)} %ct_hbm.1) | copy-start | bytes 6291460
  3.8 1.2 %copy-start.2 = (bf16[8192,64]{0,1:T(8,128)(2,1)S(1)}, bf16[8192,64]{0,1:T(8,128)(2,1)}, u32[]{:S(2)}) copy-start(bf16[8192,64]{0,1:T(8,128)(2,1)} %param.16) | copy-start | bytes 3145732
  5.0 1.2 %copy-start.3 = (bf16[64,8192]{1,0:T(8,128)(2,1)S(1)}, bf16[64,8192]{1,0:T(8,128)(2,1)}, u32[]{:S(2)}) copy-start(bf16[64,8192]{1,0:T(8,128)(2,1)} %up_hbm.1) | copy-start | bytes 3145732
  6.3 1.0 %copy-start.4 = (bf16[32,8192]{1,0:T(8,128)(2,1)S(1)}, bf16[32,8192]{1,0:T(8,128)(2,1)}, u32[]{:S(2)}) copy-start(bf16[32,8192]{1,0:T(8,128)(2,1)} %xv_hbm.1) | copy-start | bytes 1572868
  7.3 1.0 %copy-start.5 = (bf16[32,8192]{1,0:T(8,128)(2,1)S(1)}, bf16[32,8192]{1,0:T(8,128)(2,1)}, u32[]{:S(2)}) copy-start(bf16[32,8192]{1,0:T(8,128)(2,1)} %ctv_hbm.1) | copy-start | bytes 1572868
  8.4 0.8 copy-start.6
  9.1 0.7 copy-start.9
  9.8 0.7 copy-start.10
  10.4 11.3 %copy-start.7 = (bf16[1,128,128]{2,1,0:T(8,128)(2,1)S(1)}, bf16[1,128,128]{2,1,0:T(8,128)(2,1)}, u32[]{:S(2)}) copy-start(bf16[1,128,128]{2,1,0:T(8,128)(2,1)} %m_hbm.1) | copy-start | bytes 98308
  10.4 11.3 %copy-start.8 = (bf16[1,128,128]{2,1,0:T(8,128)(2,1)S(1)}, bf16[1,128,128]{2,1,0:T(8,128)(2,1)}, u32[]{:S(2)}) copy-start(bf16[1,128,128]{2,1,0:T(8,128)(2,1)} %v_hbm.1) | copy-start | bytes 98308
